TPU v7x, 128 devices: a whole 4x4x4 slice. The times are simulated.
128 devices in a mesh: req: 4 (over z), seq: 32 (over x, y, core).
Axes of the slice: x: 4, y: 4, z: 4, core: 2. Of those that a mesh axis runs over, the one named last changes fastest.
Arguments:
- tokens: bfloat16 [4, 2048, 3584], P('req', 'seq'), may hold values from -6 to 6
- w_z: bfloat16 [3584, 7168], P('req', 'seq')
- w_x: bfloat16 [3584, 7168], P('req', 'seq'), may hold values from -0.09375 to 0.09375
- w_bc: bfloat16 [3584, 256], replicated, may hold values from -0.09375 to 0.09375
- w_dt: bfloat16 [3584, 112], replicated, may hold values from -0.09375 to 0.09375
- dt_bias: float32 [112], replicated, may hold values from -2 to 0
- a_rate: float32 [112], replicated, may hold values from 0.00024414062 to 0.2
- conv_weight: float32 [4, 7424], replicated, may hold values from -3 to 3
- conv_bias: float32 [7424], replicated, may hold values from -3 to 3
- d_skip: float32 [112], replicated, may hold values from 0.5 to 1.5
- norm_gain: float32 [7168], replicated, may hold values from 0.5 to 1.5
- lengths: int32 [4], P('req'), may hold values from 512 to 2048, as said below
Outputs:
- mixed: bfloat16 [4, 2048, 7168], P('req', 'seq')
Inputs may be any that keep to these rules, and one draw needn't show every extreme that they name: `lengths`: each prompt has at least 512 valid positions, and the longest fills all 2048.
All inputs are finite; a program needn't handle non-finite values.
Results may differ from a plain program's by a relative error of at most 0.0055.
Values may be sent and summed in bfloat16 or wider, within the bound.
No kernel may reach another device: no remote copies, remote signals or barrier semaphores. Data moves between devices by JAX's collectives and lax.ppermute only.
A program may use at most 320 MiB of HBM per device.

v0:
```python
import jax
import jax.numpy as jnp
from jax import lax
from jax.sharding import PartitionSpec as P

STATE = 64
GROUPS = 2


PRECISE = lax.Precision.HIGHEST


def from_behind(block, axis, distance):
    devices = range(lax.axis_size(axis))
    route = [(i - distance, i) for i in devices if i - distance in devices]
    return lax.ppermute(block, axis, route)


def prefix(shard, axis, combine, identity):
    size, position = (lax.axis_size(axis), lax.axis_index(axis))
    everything = jax.tree.map(lambda part: lax.all_gather(part, axis), shard)
    start = jax.tree.map(
        lambda part, zero: jnp.broadcast_to(jnp.asarray(zero, part.dtype), part.shape),
        shard,
        identity,
    )

    def hop(k, before):
        reached = k < position
        new = combine(before, jax.tree.map(lambda part: part[k], everything))
        return jax.tree.map(lambda a, b: jnp.where(reached, a, b), new, before)

    return lax.fori_loop(0, size, hop, start)


def local_block(x_heads, b_proj, c_proj, step_size, log_decay):
    per_group = x_heads.shape[1] // b_proj.shape[1]
    block_len = x_heads.shape[0]
    running = jnp.cumsum(log_decay, axis=0)
    causal_mask = jnp.arange(block_len)[:, None] >= jnp.arange(block_len)[None, :]
    gaps = running.T[:, :, None] - running.T[:, None, :]
    decay_mask = jnp.where(causal_mask[None], jnp.exp(jnp.minimum(gaps, 0.0)), 0.0)
    affinity = jnp.einsum("ign,jgn->gij", c_proj, b_proj, precision=PRECISE)
    mixing = decay_mask * jnp.repeat(affinity, per_group, axis=0) * step_size.T[:, None, :]
    intra_out = jnp.einsum("hij,jhp->ihp", mixing, x_heads, precision=PRECISE)
    b_heads = jnp.repeat(b_proj, per_group, axis=1)
    tail_weight = jnp.exp(running[-1][None, :] - running) * step_size
    block_state = jnp.einsum(
        "jhp,jhn->hpn", x_heads * tail_weight[:, :, None], b_heads, precision=PRECISE
    )
    return (intra_out, block_state, running)


def finish_block(
    x_heads, c_proj, running, intra_out, state_in, gate_in, d_skip, norm_gain, valid_rows
):
    per_group = x_heads.shape[1] // c_proj.shape[1]
    num_rows = x_heads.shape[0]
    inner_width = norm_gain.shape[0]
    c_heads = jnp.repeat(c_proj, per_group, axis=1)
    carried = jnp.exp(running)[:, :, None] * jnp.einsum(
        "ihn,hpn->ihp", c_heads, state_in, precision=PRECISE
    )
    result = intra_out + carried + d_skip[None, :, None] * x_heads
    gated = result.reshape(num_rows, inner_width) * jax.nn.silu(gate_in.astype(jnp.float32))
    grouped = gated.reshape(num_rows, GROUPS, inner_width // GROUPS)
    inv_scale = lax.rsqrt(jnp.mean(grouped * grouped, axis=2, keepdims=True) + 1e-05)
    normed = (grouped * inv_scale).reshape(num_rows, inner_width) * norm_gain[None, :]
    return jnp.where(valid_rows[:, None], normed, 0.0).astype(jnp.bfloat16)


def combine_states(earlier_part, later_part):
    return (
        earlier_part[0] + later_part[0],
        jnp.exp(later_part[0])[:, None, None] * earlier_part[1] + later_part[1],
    )


def position_mix(
    stacked, bc_proj, dt_raw, dt_bias, a_rate, conv_weight, conv_bias, d_skip, norm_gain, lengths
):
    regrouped = lax.all_to_all(stacked, "seq", split_axis=0, concat_axis=2, tiled=True)
    gate_in = regrouped[:, 0]
    x_in = regrouped[:, 1]
    num_rows = gate_in.shape[0]
    inner_width = norm_gain.shape[0]
    num_heads = a_rate.shape[0]
    head_size = inner_width // num_heads
    conv_taps = conv_weight.shape[0]
    proj_width = bc_proj.shape[1] // 2
    xbc = jnp.concatenate([x_in, bc_proj], axis=1)
    rim_rows = from_behind(xbc[num_rows - (conv_taps - 1) :], "seq", 1)
    padded = jnp.concatenate([rim_rows, xbc], axis=0).astype(jnp.float32)
    conv_sum = conv_bias[None, :] + jnp.zeros(xbc.shape, jnp.float32)
    for offset in range(conv_taps):
        conv_sum = conv_sum + conv_weight[offset][None, :] * padded[offset : offset + num_rows]
    conved = lax.optimization_barrier(jax.nn.silu(conv_sum).astype(jnp.bfloat16)).astype(
        jnp.float32
    )
    x_heads = conved[:, :inner_width].reshape(num_rows, num_heads, head_size)
    b_proj = conved[:, inner_width : inner_width + proj_width].reshape(num_rows, GROUPS, STATE)
    c_proj = conved[:, inner_width + proj_width :].reshape(num_rows, GROUPS, STATE)
    step_size = jax.nn.softplus(dt_raw.astype(jnp.float32) + dt_bias[None, :])
    log_decay = -step_size * a_rate[None, :]
    first_row = lax.axis_index("seq") * num_rows
    valid_rows = first_row + jnp.arange(num_rows, dtype=jnp.int32) < lengths[0]
    intra_out, block_state, running = local_block(x_heads, b_proj, c_proj, step_size, log_decay)
    total_log = running[-1]
    identity = (jnp.zeros_like(total_log), jnp.zeros_like(block_state))
    carried_log, state_in = prefix((total_log, block_state), "seq", combine_states, identity)
    return finish_block(
        x_heads, c_proj, running, intra_out, state_in, gate_in, d_skip, norm_gain, valid_rows
    )


def local(
    tokens,
    w_z,
    w_x,
    w_bc,
    w_dt,
    dt_bias,
    a_rate,
    conv_weight,
    conv_bias,
    d_skip,
    norm_gain,
    lengths,
):
    own_rows = tokens[0]
    z_columns, x_columns = (
        lax.all_gather(w_z, "req", axis=0, tiled=True),
        lax.all_gather(w_x, "req", axis=0, tiled=True),
    )
    shard_piece = lax.all_gather(own_rows, "seq", axis=0, tiled=True)
    gate_part = jnp.dot(shard_piece, z_columns, preferred_element_type=jnp.float32).astype(
        jnp.bfloat16
    )
    input_part = jnp.dot(shard_piece, x_columns, preferred_element_type=jnp.float32).astype(
        jnp.bfloat16
    )
    stacked = jnp.stack([gate_part, input_part], axis=1)
    bc_proj = jnp.dot(own_rows, w_bc, preferred_element_type=jnp.float32).astype(jnp.bfloat16)
    dt_raw = jnp.dot(own_rows, w_dt, preferred_element_type=jnp.float32).astype(jnp.bfloat16)
    operands = (
        stacked,
        bc_proj,
        dt_raw,
        dt_bias,
        a_rate,
        conv_weight,
        conv_bias,
        d_skip,
        norm_gain,
        lengths,
    )
    mixed = position_mix(*operands)
    return mixed[None]


def solution(mesh):
    placed = (
        P("req", "seq", None),
        P("req", "seq"),
        P("req", "seq"),
        P(),
        P(),
        P(),
        P(),
        P(),
        P(),
        P(),
        P(),
        P("req"),
    )
    return jax.shard_map(
        local, mesh=mesh, in_specs=placed, out_specs=P("req", "seq", None), check_vma=False
    )
```

profile of v0, /device:TPU:1, one launch (start us, length us, event | category | flops | bytes accessed | tf_op | source)
XLA Modules:
  0.0 760.6 jit_solution(18271068102787974957)
XLA Ops:
  8.7 30.3 %all-gather.10.cloned.1.call-done = bf16[3584,224]{0,1:T(8,128)(2,1)} async-done(((bf16[896,224]{0,1:T(8,128)(2,1)}), bf16[3584,224]{0,1:T(8,128)(2,1)}) %all-gather.10.cloned.1.call-update) | async-done | bytes 1605648 | tf_op jit(solution)/shard_map/all_gather | solution.py:133
  39.0 70.3 %all-gather.12.cloned.1.call-done = bf16[1,2048,3584]{2,1,0:T(8,128)(2,1)} async-done(((bf16[1,64,3584]{2,1,0:T(8,128)(2,1)}), bf16[1,2048,3584]{2,1,0:T(8,128)(2,1)}) %all-gather.12.cloned.1.call-update) | async-done | bytes 14680080 | tf_op jit(solution)/shard_map/all_gather | solution.py:135
  109.3 10.0 %fusion.16 = bf16[2048,1,224]{0,2,1:T(8,128)(2,1)S(1)} fusion(bf16[3584,224]{0,1:T(8,128)(2,1)} %all-gather.10.cloned.1.call-done, bf16[1,2048,3584]{2,1,0:T(8,128)(2,1)} %all-gather.12.cloned.1.call-done), kind=kOutput, calls=%fused_computation.17 | convolution fusion | flops 3288793088 | bytes 17203200 | tf_op jit(solution)/shard_map/dot_general | solution.py:139
  119.3 17.7 %all-gather.8.cloned.1.call-done = bf16[3584,224]{0,1:T(8,128)(2,1)} async-done(((bf16[896,224]{0,1:T(8,128)(2,1)}), bf16[3584,224]{0,1:T(8,128)(2,1)}) %all-gather.8.cloned.1.call-update) | async-done | bytes 1605648 | tf_op jit(solution)/shard_map/all_gather | solution.py:132
  137.0 9.9 %fusion.19 = bf16[2048,1,224]{0,2,1:T(8,128)(2,1)S(1)} fusion(bf16[3584,224]{0,1:T(8,128)(2,1)} %all-gather.8.cloned.1.call-done, bf16[1,2048,3584]{2,1,0:T(8,128)(2,1)} %all-gather.12.cloned.1.call-done), kind=kOutput, calls=%fused_computation.18 | convolution fusion | flops 3288793088 | bytes 17203200 | tf_op jit(solution)/shard_map/dot_general | solution.py:136
  148.3 6.2 copy.89
  154.5 7.9 %all-to-all-start = ((bf16[2048,2,224]{2,1,0:T(2,128)(2,1)}), bf16[2048,2,224]{2,1,0:T(2,128)(2,1)}, u32[]{:S(2)}, u32[]{:S(2)}) async-start(bf16[2048,2,224]{2,1,0:T(2,128)(2,1)} %copy.89), calls=%async_computation | async-start | bytes 4194304 | tf_op jit(solution)/shard_map/all_to_all | solution.py:82
  163.5 27.3 %all-to-all-done = bf16[2048,2,224]{2,1,0:T(2,128)(2,1)} async-done(((bf16[2048,2,224]{2,1,0:T(2,128)(2,1)}), bf16[2048,2,224]{2,1,0:T(2,128)(2,1)}, u32[]{:S(2)}, u32[]{:S(2)}) %all-to-all-start) | async-done | bytes 1835040 | tf_op jit(solution)/shard_map/all_to_all | solution.py:82
  213.0 6.0 fusion.8
  220.0 24.4 %all-gather.2 = f32[32,1,112]{2,1,0:T(1,128)S(1)} all-gather(f32[1,1,112]{2,1,0:T(1,128)S(1)} %get-tuple-element.141), channel_id=1, replica_groups=mesh['req'=4,'seq'=32] {'seq'}, dimensions={0}, use_global_device_ids=true | all-gather | bytes 14784 | tf_op jit(solution)/shard_map/all_gather | solution.py:21
  256.1 294.6 %all-gather.14.cloned.1.call-done = f32[3584,64,64]{2,1,0:T(8,128)} async-done(((f32[112,64,64]{2,1,0:T(8,128)}), f32[3584,64,64]{2,1,0:T(8,128)}) %all-gather.14.cloned.1.call-update) | async-done | bytes 58720272 | tf_op jit(solution)/shard_map/all_gather | solution.py:21
  550.7 179.3 %while.14 = (s32[]{:T(128)}, f32[112,64,64]{2,1,0:T(8,128)}, s32[]{:T(128)}, f32[32,112]{1,0:T(8,128)S(1)}, f32[32,112,64,64]{3,2,1,0:T(8,128)}, /*index=5*/s32[]{:T(128)}, s32[]{:T(128)}) while((s32[]{:T(128)}, f32[112,64,64]{2,1,0:T(8,128)}, s32[]{:T(128)}, f32[32,112]{1,0:T(8,128)S(1)}, f32[32,112,64,64]{3,2,1,0:T(8,128)}, ...), condition=%wide.region_2.3_spmd.clone, body=%wide.region_1.2_spmd.clone.sunk | while | flops 1835012 | bytes 5506481 | solution.py:33
  555.3 5.6 fusion.58
  560.9 5.6 fusion.58
  566.5 5.6 fusion.58
  577.8 5.6 fusion.58
  583.4 5.6 fusion.58
  589.1 5.6 fusion.58
  606.0 5.7 fusion.58
  611.7 5.7 fusion.58
  628.6 5.6 fusion.58
  696.2 5.7 fusion.58
  701.9 5.6 fusion.58
  732.1 10.9 %multiply_reduce_fusion = (f32[64,112]{0,1:T(8,128)S(1)}, f32[64,112,64]{0,2,1:T(8,128)}) fusion(f32[64,112,64]{0,2,1:T(8,128)} %bitcast.121, f32[64,112,64]{0,2,1:T(8,128)} %bitcast.116, f32[112]{0:T(128)S(1)} %copy-done.13, f32[112,64,64]{2,1,0:T(8,128)S(1)} %copy-done.2, f32[64,112,64]{2,0,1:T(8,128)S(1)} %bitcast.120, f32[64,112]{0,1:T(8,128)S(1)} %copy.98, ...), kind=kOutput, calls=%fused_computation.12 | convolution fusion | flops 357360640 | bytes 11067840 | tf_op jit(solution)/shard_map/ihn,hpn->ihp/dot_general | solution.py:61
  (138 shorter events, 169.0 us)
Async XLA Ops:
  6.5 156.5 %copy-start = (bf16[3584,256]{1,0:T(8,128)(2,1)S(1)}, bf16[3584,256]{1,0:T(8,128)(2,1)}, u32[]{:S(2)}) copy-start(bf16[3584,256]{1,0:T(8,128)(2,1)} %param.17) | copy-start | bytes 5505028
  6.5 32.5 %all-gather.10.cloned.1.call-start = ((), (), s32[]{:S(2)}) async-start(), calls=%async_computation.2 | async-start | bytes 2007040 | tf_op jit(solution)/shard_map/all_gather | solution.py:133
  7.3 102.0 %all-gather.12.cloned.1.call-start = ((), (), s32[]{:S(2)}) async-start(), calls=%async_computation.3 | async-start | bytes 15138816 | tf_op jit(solution)/shard_map/all_gather | solution.py:135
  8.0 128.9 %all-gather.8.cloned.1.call-start = ((), (), s32[]{:S(2)}) async-start(), calls=%async_computation.1 | async-start | bytes 2007040 | tf_op jit(solution)/shard_map/all_gather | solution.py:132
  154.4 8.0 %copy-start.6 = (bf16[1,64,3584]{2,1,0:T(8,128)(2,1)S(1)}, bf16[1,64,3584]{2,1,0:T(8,128)(2,1)}, u32[]{:S(2)}) copy-start(bf16[1,64,3584]{2,1,0:T(8,128)(2,1)} %param.14) | copy-start | bytes 1376260
  154.4 8.0 %copy-start.7 = (bf16[3584,112]{0,1:T(8,128)(2,1)S(1)}, bf16[3584,112]{0,1:T(8,128)(2,1)}, u32[]{:S(2)}) copy-start(bf16[3584,112]{0,1:T(8,128)(2,1)} %param.18) | copy-start | bytes 2408452
  154.4 8.0 %copy-start.11 = (f32[112]{0:T(128)S(1)}, f32[112]{0:T(128)}, u32[]{:S(2)}) copy-start(f32[112]{0:T(128)} %param.19) | copy-start | bytes 1348
  154.5 8.4 %copy-start.12 = (f32[112]{0:T(128)S(1)}, f32[112]{0:T(128)}, u32[]{:S(2)}) copy-start(f32[112]{0:T(128)} %param.20) | copy-start | bytes 1348
  154.5 36.3 %all-to-all-start = ((bf16[2048,2,224]{2,1,0:T(2,128)(2,1)}), bf16[2048,2,224]{2,1,0:T(2,128)(2,1)}, u32[]{:S(2)}, u32[]{:S(2)}) async-start(bf16[2048,2,224]{2,1,0:T(2,128)(2,1)} %copy.89), calls=%async_computation | async-start | bytes 4194304 | tf_op jit(solution)/shard_map/all_to_all | solution.py:82
  162.4 388.4 %all-gather.14.cloned.1.call-start = ((), (), s32[]{:S(2)}) async-start(), calls=%async_computation.4 | async-start | bytes 121110528 | tf_op jit(solution)/shard_map/all_gather | solution.py:21
  199.5 1.8 copy-start.4
  199.5 4.0 copy-start.8
  201.3 3.5 copy-start.9
  201.4 3.2 collective-permute-start
  211.0 2.0 copy-start.3
  249.7 1.5 copy-start.5
  730.1 2.0 copy-start.2
  730.1 2.0 copy-start.13
  746.5 3.7 copy-start.10
  746.5 7.6 copy-start.1
Sparse Core Ops, SparseCore 0:
  9.0 29.9 all-gather.9
  41.3 67.9 all-gather.11
  111.0 25.9 all-gather.7
  219.1 331.5 all-gather.13
where the time goes:
time: 761 us
  waiting for transfers between devices  443 us (58%)
  other arithmetic  189 us (25%)
  matrix products  42.6 us (6%)
  local copies, waits for them, and re-layouts  37.7 us (5%)
  blocking collectives  24.4 us (3%)
  between operations  14.1 us (2%)
  starting transfers between devices  10.1 us (1%)
    all_gather x1, waiting for transfers between devices, prefix(): everything = jax.tree.map(lambda part: lax.all_gather(part, axis), shard)  295 us
    select_n x32, other arithmetic, hop(): return jax.tree.map(lambda a, b: jnp.where(reached, a, b), new, before)  179 us
    all_gather x1, waiting for transfers between devices, local(): shard_piece = lax.all_gather(own_rows, 'seq', axis=0, tiled=True)  70.3 us
    all_gather x1, waiting for transfers between devices, local(): lax.all_gather(w_x, 'req', axis=0, tiled=True)  30.3 us
    all_to_all x1, waiting for transfers between devices, position_mix(): lax.all_to_all(stacked, 'seq', split_axis=0, concat_axis=2, tiled=True)  27.3 us
    all_gather x1, blocking collectives, prefix(): everything = jax.tree.map(lambda part: lax.all_gather(part, axis), shard)  24.4 us
    all_gather x1, waiting for transfers between devices, local(): lax.all_gather(w_z, 'req', axis=0, tiled=True)  17.7 us
  transfers between devices with their start and end apart: 6, of which 6 were waited for; matrix products, arithmetic and copies ran while one was open for 3% of the time, Pallas kernels for 0%

commit v1 on v0

v1 whole, which is shorter than its diff:
```python
import functools

import jax
import jax.numpy as jnp
from jax import lax
from jax.experimental import pallas as pl
from jax.experimental.pallas import tpu as pltpu
from jax.sharding import PartitionSpec as P

STATE = 64
GROUPS = 2
HEAD = 64
CHUNK = 128
ROWS = 512
LANES = 128

F32 = jnp.float32
BF16 = jnp.bfloat16
NT = (((1,), (1,)), ((), ()))
NN = (((1,), (0,)), ((), ()))
TN = (((0,), (0,)), ((), ()))


def mm(a, b, dims):
    return lax.dot_general(a, b, dims, preferred_element_type=F32)


def halves(v):
    high = v.astype(BF16)
    return high, (v - high.astype(F32)).astype(BF16)


def silu(v):
    return v / (1.0 + jnp.exp(-v))


def mixer_kernel(
    shift_ref,
    tok_ref,
    w_ref,
    rest_ref,
    convx_ref,
    convr_ref,
    bias_ref,
    rate_ref,
    skip_ref,
    out_ref,
    state,
    z_buf,
    x_buf,
    r_buf,
    dt_buf,
):
    width = out_ref.shape[1]
    rows = tok_ref.shape[0]
    parts, _, depth = w_ref.shape
    half = 2 * STATE

    @pl.when(pl.program_id(0) == 0)
    def _():
        state[...] = jnp.zeros_like(state)
        x_buf[0:8] = jnp.zeros((8, width), F32)
        r_buf[0:8] = jnp.zeros((8, half), F32)

    z, x, rest = (0.0, 0.0, 0.0)
    for k in range(parts):
        t = tok_ref[:, k * depth : (k + 1) * depth]
        z = z + mm(t, w_ref[k, 0:width], NT)
        x = x + mm(t, w_ref[k, width : 2 * width], NT)
        rest = rest + mm(t, rest_ref[:, k * depth : (k + 1) * depth], NT)
    z_buf[...] = z.astype(BF16).astype(F32)
    x_buf[8 : 8 + rows] = x.astype(BF16).astype(F32)
    rest = rest.astype(BF16).astype(F32)
    r_buf[8 : 8 + rows] = rest[:, :half]
    dt_buf[...] = rest[:, half:]

    row = lax.broadcasted_iota(jnp.int32, (CHUNK, CHUNK), 0)
    col = lax.broadcasted_iota(jnp.int32, (CHUNK, CHUNK), 1)
    causal = row >= col
    tril = jnp.where(causal, 1.0, 0.0).astype(F32)
    lane_head = (lax.broadcasted_iota(jnp.int32, (1, width), 1) + shift_ref[0]) // HEAD

    def conv(window, taps_ref):
        total = taps_ref[4:5, :]
        for k in range(4):
            total = total + taps_ref[k : k + 1, :] * window[5 + k : 5 + k + CHUNK]
        return silu(total).astype(BF16)

    def spread(columns):
        out = columns[:, 0:1]
        for h in range(1, 4):
            out = jnp.where(lane_head == h, columns[:, h : h + 1], out)
        return out

    def step(c, carry):
        start = pl.multiple_of(c * CHUNK, CHUNK)
        xb = conv(x_buf[pl.ds(start, CHUNK + 8), :], convx_ref)
        bc = conv(r_buf[pl.ds(start, CHUNK + 8), :], convr_ref).astype(F32)
        b = bc[:, :STATE].astype(BF16)
        c_ = bc[:, STATE:].astype(BF16)
        xf = xb.astype(F32)
        pre = dt_buf[pl.ds(start, CHUNK), :] + bias_ref[...]
        size = jnp.maximum(pre, 0.0) + jnp.log1p(jnp.exp(-jnp.abs(pre)))
        decay = -size * rate_ref[...]
        running = lax.dot_general(
            tril, decay, NN, precision=lax.Precision.HIGHEST, preferred_element_type=F32
        )
        run_t = jnp.transpose(running)
        size_t = jnp.transpose(size)
        affinity = jnp.where(causal, mm(c_, b, NT), 0.0)
        intra = jnp.zeros((CHUNK, width), F32)
        for h in range(4):
            gap = running[:, h : h + 1] - run_t[h : h + 1, :]
            mix = affinity * jnp.exp(jnp.minimum(gap, 0.0)) * size_t[h : h + 1, :]
            high, low = halves(mix)
            own = jnp.where(lane_head == h, xf, 0.0).astype(BF16)
            intra = intra + mm(high, own, NN) + mm(low, own, NN)
        run_wide = spread(running)
        size_wide = spread(size)
        last = run_wide[CHUNK - 1 : CHUNK, :]
        old = state[...]
        high, low = halves(old)
        carried = jnp.exp(run_wide) * (mm(c_, high, NN) + mm(c_, low, NN))
        high, low = halves(xf * (jnp.exp(last - run_wide) * size_wide))
        state[...] = jnp.exp(last) * old + (mm(b, high, TN) + mm(b, low, TN))
        result = intra + carried + skip_ref[...] * xf
        gated = result * silu(z_buf[pl.ds(start, CHUNK), :])
        out_ref[pl.ds(start, CHUNK), :] = gated.astype(BF16)
        return carry

    lax.fori_loop(0, rows // CHUNK, step, 0)
    x_buf[0:8] = x_buf[rows : rows + 8]
    r_buf[0:8] = r_buf[rows : rows + 8]


def norm_kernel(valid_ref, in_ref, gain_ref, out_ref):
    pieces, rows, width = in_ref.shape
    per = pieces // GROUPS
    keep = lax.broadcasted_iota(jnp.int32, (rows, 1), 0) < valid_ref[0]
    for g in range(GROUPS):
        total = jnp.zeros((rows, width), F32)
        for d in range(per):
            v = in_ref[g * per + d].astype(F32)
            total = total + v * v
        mean = jnp.sum(total, axis=1, keepdims=True) / (per * width)
        scale = lax.rsqrt(mean + 1e-05)
        for d in range(g * per, (g + 1) * per):
            v = in_ref[d].astype(F32) * scale * gain_ref[d : d + 1, :]
            out_ref[:, d * width : (d + 1) * width] = jnp.where(keep, v, 0.0).astype(BF16)


def mixer(tokens, weights, rest, convx, convr, bias, rate, skip, shift):
    length, d_model = tokens.shape
    width = skip.shape[1]
    whole = lambda a: pl.BlockSpec(
        a.shape, lambda i: (0,) * a.ndim, pipeline_mode=pl.Buffered(1)
    )
    return pl.pallas_call(
        mixer_kernel,
        grid=(length // ROWS,),
        in_specs=[
            pl.BlockSpec(memory_space=pltpu.SMEM),
            pl.BlockSpec((ROWS, d_model), lambda i: (i, 0)),
            whole(weights),
            whole(rest),
            whole(convx),
            whole(convr),
            whole(bias),
            whole(rate),
            whole(skip),
        ],
        out_specs=pl.BlockSpec((ROWS, width), lambda i: (i, 0)),
        out_shape=jax.ShapeDtypeStruct((length, width), BF16),
        scratch_shapes=[
            pltpu.VMEM((STATE, width), F32),
            pltpu.VMEM((ROWS, width), F32),
            pltpu.VMEM((ROWS + 8, width), F32),
            pltpu.VMEM((ROWS + 8, 2 * STATE), F32),
            pltpu.VMEM((ROWS, LANES), F32),
        ],
        compiler_params=pltpu.CompilerParams(vmem_limit_bytes=48 * 1024 * 1024),
        name="mixer",
    )(shift, tokens, weights, rest, convx, convr, bias, rate, skip)


def local(
    tokens,
    w_z,
    w_x,
    w_bc,
    w_dt,
    dt_bias,
    a_rate,
    conv_weight,
    conv_bias,
    d_skip,
    norm_gain,
    lengths,
):
    own_rows = tokens[0]
    num_rows, d_model = own_rows.shape
    width = w_z.shape[1]
    seq = lax.axis_size("seq")
    me = lax.axis_index("seq")
    inner = width * seq

    both = jnp.concatenate([w_z.T, w_x.T], axis=0)
    weights = lax.all_gather(both, "req", axis=0)
    everyone = lax.all_gather(own_rows, "seq", axis=0, tiled=True)

    first = me * width
    head = first // HEAD
    group = me * GROUPS // seq
    cut = lambda a, at, n: lax.dynamic_slice_in_dim(a, at, n, axis=a.ndim - 1)
    pick = lambda a: jnp.concatenate(
        [cut(a, group * STATE, STATE), cut(a, (GROUPS + group) * STATE, STATE)], axis=-1
    )
    dt_rows = lax.dynamic_slice_in_dim(w_dt.T, head, 4, axis=0)
    rest = jnp.concatenate(
        [pick(w_bc).T, dt_rows, jnp.zeros((LANES - 4, d_model), BF16)], axis=0
    )
    taps = jnp.concatenate([conv_weight, conv_bias[None]], axis=0)
    convx = cut(taps, first, width)
    convr = pick(taps[:, inner:])
    pad = lambda a: jnp.pad(cut(a, head, 4), (0, LANES - 4))[None]
    shift = first - head * HEAD
    skip = cut(jnp.repeat(d_skip, HEAD), first, width)[None]
    gated = mixer(
        everyone, weights, rest, convx, convr, pad(dt_bias), pad(a_rate), skip, shift[None]
    )
    pieces = lax.all_to_all(
        gated.reshape(seq, num_rows, width), "seq", split_axis=0, concat_axis=0, tiled=True
    )
    valid = lengths - me * num_rows
    mixed = pl.pallas_call(
        norm_kernel,
        in_specs=[
            pl.BlockSpec(memory_space=pltpu.SMEM),
            pl.BlockSpec(memory_space=pltpu.VMEM),
            pl.BlockSpec(memory_space=pltpu.VMEM),
        ],
        out_specs=pl.BlockSpec(memory_space=pltpu.VMEM),
        out_shape=jax.ShapeDtypeStruct((num_rows, inner), BF16),
        name="norm",
    )(valid, pieces, norm_gain.reshape(seq, width))
    return mixed[None]


def solution(mesh):
    placed = (
        P("req", "seq", None),
        P("req", "seq"),
        P("req", "seq"),
        P(),
        P(),
        P(),
        P(),
        P(),
        P(),
        P(),
        P(),
        P("req"),
    )
    return jax.shard_map(
        local, mesh=mesh, in_specs=placed, out_specs=P("req", "seq", None), check_vma=False
    )
```

time: 761 us -> 189 us (0.25)
  waiting for transfers between devices: 443 us -> 126 us
  other arithmetic: 189 us -> 2.71 us
  matrix products: 42.6 us -> 0 us
  Pallas kernels: 0 us -> 32.2 us
  local copies, waits for them, and re-layouts: 37.7 us -> 7.85 us
  blocking collectives: 24.4 us -> 0 us
    all_gather x4 -> x2, waiting for transfers between devices: 413 us -> 109 us  [the longest x1 70.5 us: local(): everyone = lax.all_gather(own_rows, 'seq', axis=0, tiled=True)]
    select_n x32 -> x0, other arithmetic: 179 us -> none  [hop(): return jax.tree.map(lambda a, b: jnp.where(reached, a, b), new, before)]
    dot_general x8 -> x0, matrix products: 42.6 us -> none  [the longest x1 10.9 us: finish_block(): jnp.einsum('ihn,hpn->ihp', c_heads, state_in, precision=PRECISE)]
    pallas_call x0 -> x2, Pallas kernels: none -> 32.2 us  [the longest x1 29.5 us: mixer(): pl.pallas_call(mixer_kernel, grid=(length // ROWS,), in_specs=[pl.BlockSp...]
    all_gather x1 -> x0, blocking collectives: 24.4 us -> none  [prefix(): everything = jax.tree.map(lambda part: lax.all_gather(part, axis), shard)]
    all_to_all x1, waiting for transfers between devices: 27.3 us -> 15.6 us  [local(): lax.all_to_all(gated.reshape(seq, num_rows, width), 'seq', split_axis=0,...]
    all_to_all x3 -> x0, local copies, waits for them, and re-layouts: 8.73 us -> none  [position_mix(): lax.all_to_all(stacked, 'seq', split_axis=0, concat_axis=2, tiled=True)]
  transfers between devices with their start and end apart: 6 -> 3, of which waited for: 6 -> 3; matrix products, arithmetic and copies ran while one was open for 3% -> 2% of each run, Pallas kernels for 0% -> 0%
where the time goes in v1:
time: 189 us; the launch traced here: 188 us
  waiting for transfers between devices  126 us (67%)
  Pallas kernels  32.2 us (17%)
  between operations  14.2 us (8%)
  local copies, waits for them, and re-layouts  7.85 us (4%)
  starting transfers between devices  5.59 us (3%)
  other arithmetic  2.71 us (1%)
    all_gather x1, waiting for transfers between devices, local(): everyone = lax.all_gather(own_rows, 'seq', axis=0, tiled=True)  70.5 us
    all_gather x1, waiting for transfers between devices, local(): weights = lax.all_gather(both, 'req', axis=0)  38.9 us
    pallas_call x1, Pallas kernels, mixer(): pl.pallas_call(mixer_kernel, grid=(length // ROWS,), in_specs=[pl.BlockSp...  29.5 us
    all_to_all x1, waiting for transfers between devices, local(): lax.all_to_all(gated.reshape(seq, num_rows, width), 'seq', split_axis=0,...  15.6 us
    all_to_all x1, starting transfers between devices, local(): lax.all_to_all(gated.reshape(seq, num_rows, width), 'seq', split_axis=0,...  5.55 us
    unnamed x22, local copies, waits for them, and re-layouts  4.61 us
  transfers between devices with their start and end apart: 3, of which 3 were waited for; matrix products, arithmetic and copies ran while one was open for 2% of the time, Pallas kernels for 0%

profile of v1, /device:TPU:1, one launch (start us, length us, event | category | flops | bytes accessed | tf_op | source)
XLA Modules:
  0.0 188.2 jit_solution(11496594205429034974)
XLA Ops:
  6.5 2.1 %pad_maximum_fusion = bf16[448,896]{1,0:T(8,128)(2,1)} fusion(bf16[224,896]{1,0:T(8,128)(2,1)} %bitcast.21, bf16[224,896]{1,0:T(8,128)(2,1)} %bitcast.22), kind=kLoop, calls=%fused_computation.2 | loop fusion | flops 1605632 | bytes 1605632 | tf_op jit(solution)/shard_map/concatenate | solution.py:207
  8.8 0.7 all-gather.5.cloned.1.call-update
  9.5 2.0 %constant_dynamic-slice_fusion.1 = (bf16[3584,64]{1,0:T(8,128)(2,1)S(1)}, bf16[3584,64]{1,0:T(8,128)(2,1)S(1)}) fusion(bf16[3584,256]{1,0:T(8,128)(2,1)} %param.15, s32[]{:T(128)S(6)} %select_n.29, s32[]{:T(128)S(6)} %select_n.30), kind=kLoop, calls=%fused_computation.11 | loop fusion | bytes 1835016 | tf_op jit(solution)/shard_map/dynamic_slice | solution.py:214
  11.6 0.3 copy.17
  11.9 0.3 copy.18
  12.2 0.1 copy-done.5
  12.3 0.1 dynamic_slice.33
  12.6 0.1 reshape.9
  12.6 0.1 pad.15.clone
  12.7 0.1 dynamic_slice.35
  12.8 0.1 dynamic-slice_maximum_fusion.1
  12.9 0.1 pad_maximum_fusion.1.convr_ref
  13.0 0.1 fusion.convx_ref
  13.2 0.3 maximum_maximum_fusion.rest_ref
  13.5 38.9 %all-gather.7.cloned.1.call-done = bf16[1792,896]{1,0:T(8,128)(2,1)} async-done(((bf16[448,896]{1,0:T(8,128)(2,1)}), bf16[1792,896]{1,0:T(8,128)(2,1)}) %all-gather.7.cloned.1.call-update) | async-done | bytes 3211280 | tf_op jit(solution)/shard_map/all_gather | solution.py:208
  52.3 70.5 %all-gather.5.cloned.1.call-done = bf16[1,2048,3584]{2,1,0:T(8,128)(2,1)} async-done(((bf16[1,64,3584]{2,1,0:T(8,128)(2,1)}), bf16[1,2048,3584]{2,1,0:T(8,128)(2,1)}) %all-gather.5.cloned.1.call-update) | async-done | bytes 14680080 | tf_op jit(solution)/shard_map/all_gather | solution.py:209
  122.8 1.9 %copy-done.2 = bf16[1792,896]{1,0:T(8,128)(2,1)S(1)} copy-done((bf16[1792,896]{1,0:T(8,128)(2,1)S(1)}, bf16[1792,896]{1,0:T(8,128)(2,1)}, u32[]{:S(2)}) %copy-start.2) | copy-done | bytes 3211288
  124.7 29.5 %mixer.1 = bf16[2048,224]{1,0:T(8,128)(2,1)S(1)} custom-call(s32[1]{0:T(128)} %bitcast.1.shift_ref, bf16[2048,3584]{1,0:T(8,128)(2,1)} %bitcast.20, bf16[4,448,896]{2,1,0:T(8,128)(2,1)S(1)} %bitcast.18, bf16[256,3584]{1,0:T(8,128)(2,1)S(1)} %maximum_maximum_fusion.rest_ref, f32[5,224]{1,0:T(8,128)S(1)} %fusion.convx_ref, ...), custom_call_target="tpu_custom_call" | custom-call | tf_op jit(solution)/shard_map/mixer/pallas_call | solution.py:158
  154.2 1.0 copy-done.1
  155.2 5.5 %all-to-all-start = ((bf16[32,64,224]{2,1,0:T(8,128)(2,1)}), bf16[32,64,224]{2,1,0:T(8,128)(2,1)S(1)}, u32[]{:S(2)}, u32[]{:S(2)}) async-start(bf16[32,64,224]{2,1,0:T(8,128)(2,1)} %bitcast.17), calls=%async_computation | async-start | bytes 2097152 | tf_op jit(solution)/shard_map/all_to_all | solution.py:231
  161.4 0.7 reshape.11.gain_ref
  162.1 15.6 %all-to-all-done.in_ref = bf16[32,64,224]{2,1,0:T(8,128)(2,1)S(1)} async-done(((bf16[32,64,224]{2,1,0:T(8,128)(2,1)}), bf16[32,64,224]{2,1,0:T(8,128)(2,1)S(1)}, u32[]{:S(2)}, u32[]{:S(2)}) %all-to-all-start) | async-done | bytes 917536 | tf_op jit(solution)/shard_map/all_to_all | solution.py:231
  177.7 1.0 copy-done.3
  178.6 2.7 %norm.1 = bf16[64,7168]{1,0:T(8,128)(2,1)} custom-call(s32[1]{0:T(128)S(6)} %sub.17.valid_ref, bf16[32,64,224]{2,1,0:T(8,128)(2,1)} %copy-done.3, f32[32,224]{1,0:T(8,128)} %reshape.11.gain_ref), custom_call_target="tpu_custom_call" | custom-call | tf_op jit(solution)/shard_map/norm/pallas_call | solution.py:235
  (28 shorter events, 0.4 us)
Async XLA Ops:
  6.5 6.5 %copy-start = (bf16[3584,112]{0,1:T(8,128)(2,1)S(1)}, bf16[3584,112]{0,1:T(8,128)(2,1)}, u32[]{:S(2)}) copy-start(bf16[3584,112]{0,1:T(8,128)(2,1)} %param.16) | copy-start | bytes 2408452
  6.5 45.8 %all-gather.7.cloned.1.call-start = ((), (), s32[]{:S(2)}) async-start(), calls=%async_computation.2 | async-start | bytes 4014080 | tf_op jit(solution)/shard_map/all_gather | solution.py:208
  8.7 114.1 %all-gather.5.cloned.1.call-start = ((), (), s32[]{:S(2)}) async-start(), calls=%async_computation.1 | async-start | bytes 15138816 | tf_op jit(solution)/shard_map/all_gather | solution.py:209
  11.5 0.8 copy-start.5
  11.5 0.8 copy-start.8
  11.6 0.9 copy-start.9
  11.6 0.9 copy-start.7
  11.6 1.2 copy-start.4
  122.8 1.9 %copy-start.2 = (bf16[1792,896]{1,0:T(8,128)(2,1)S(1)}, bf16[1792,896]{1,0:T(8,128)(2,1)}, u32[]{:S(2)}) copy-start(bf16[1792,896]{1,0:T(8,128)(2,1)} %all-gather.7.cloned.1.call-done) | copy-start | bytes 9633796
  154.2 1.0 copy-start.1
  155.2 6.2 %copy-start.6 = (f32[7168]{0:T(1024)S(1)}, f32[7168]{0:T(1024)}, u32[]{:S(2)}) copy-start(f32[7168]{0:T(1024)} %param.22) | copy-start | bytes 86020
  155.2 22.5 %all-to-all-start = ((bf16[32,64,224]{2,1,0:T(8,128)(2,1)}), bf16[32,64,224]{2,1,0:T(8,128)(2,1)S(1)}, u32[]{:S(2)}, u32[]{:S(2)}) async-start(bf16[32,64,224]{2,1,0:T(8,128)(2,1)} %bitcast.17), calls=%async_computation | async-start | bytes 2097152 | tf_op jit(solution)/shard_map/all_to_all | solution.py:231
  177.7 1.0 copy-start.3
Sparse Core Ops, SparseCore 0:
  9.0 43.2 all-gather.6
  54.6 68.2 all-gather.4
